TPU v7x, 256 devices: a whole 4x4x8 slice. The times are simulated.
256 devices in a mesh: freq: 8 (over z), lat: 8 (over x, y_hi), lon: 4 (over y_lo, core).
Axes of the slice: x: 4, y: 4 (y_hi: 2, y_lo: 2; y = y_hi * 2 + y_lo), z: 8, core: 2. Of those that a mesh axis runs over, the one named last changes fastest.
Arguments:
- direction: float32 [3, 32, 1024, 2048], P(None, 'freq', 'lat', 'lon'), may hold values from -6 to 6
- base_flow: float32 [2, 32, 1024, 2048], P(None, 'freq', 'lat', 'lon'), may hold values from -2 to 2
- water_depth: float32 [1024, 2048], P('lat', 'lon'), may hold values from 0.5 to 2
- drag_factor: float32 [1024, 2048], P('lat', 'lon'), may hold values from 0.2 to 2
- wet_mask: int32 [1024, 2048], P('lat', 'lon'), may hold values 0 or 1
Outputs:
- result: float32 [3, 32, 1024, 2048], P(None, 'freq', 'lat', 'lon')
All inputs are finite; a program needn't handle non-finite values. No bound on the sum of `wet_mask` on one device may be relied on, other than what follows from the above.
Results may differ from a plain program's by a relative error of at most 0.000071.
Values sent between devices are 32-bit elements; how exact they have to be, the bound alone decides.
A program may use at most 128 MiB of HBM per device.

v0:
```python
import math
import jax
import jax.numpy as jnp
from jax import lax
from jax.sharding import PartitionSpec as P

NCON = 16
NTIME = 256
LINEAR_DRAG = 0.5
GRAVITY = 1.0
OMEGA_STEP = 0.25
SPEED_SOFT = 0.01


def extended_2(block, sides, width):
    for axis, dim in sides:
        count = lax.axis_size(axis)
        forward = [(i, i + 1) for i in range(count - 1)]
        forward.append((count - 1, 0))
        backward = [(target, source) for source, target in forward]
        low = lax.ppermute(
            lax.slice_in_dim(block, block.shape[dim] - width, None, axis=dim), axis, forward
        )
        high = lax.ppermute(lax.slice_in_dim(block, 0, width, axis=dim), axis, backward)
        block = jnp.concatenate([low, block, high], axis=dim)
    return block


def samples_table(sample_count, constituents):
    sample_index = jnp.arange(sample_count, dtype=jnp.int32)
    harmonic = jnp.arange(1, constituents + 1, dtype=jnp.int32)
    wrapped_turns = sample_index[:, None] * harmonic[None, :] % sample_count
    phase_angle = wrapped_turns.astype(jnp.float32) * (2.0 * math.pi / sample_count)
    table = jnp.stack([jnp.cos(phase_angle), jnp.sin(phase_angle)], axis=2)
    return table.reshape(sample_count, 2 * constituents)


def rotation_of(row_index, total_rows):
    return 0.5 + (row_index.astype(jnp.float32) + 0.5) / total_rows


def tendency(values, angular):
    cos_sin = values.reshape((values.shape[0] // 2, 2) + values.shape[1:])
    moved = jnp.stack([angular * cos_sin[:, 1], -angular * cos_sin[:, 0]], axis=1)
    return moved.reshape(values.shape)


def linear_residual(extended, tile_rows, tile_cols, angular, rotation):

    def neighbour(plane, row_step, col_step):
        return extended[
            plane,
            :,
            1 + row_step : 1 + row_step + tile_rows,
            1 + col_step : 1 + col_step + tile_cols,
        ]

    height = neighbour(0, 0, 0)
    east = neighbour(1, 0, 0)
    north = neighbour(2, 0, 0)
    res_height = (
        tendency(height, angular)
        + neighbour(3, 0, 0)
        - neighbour(3, 0, -1)
        + neighbour(4, 0, 0)
        - neighbour(4, -1, 0)
    )
    north_mean = 0.25 * (north + neighbour(2, 0, 1) + neighbour(2, -1, 0) + neighbour(2, -1, 1))
    east_mean = 0.25 * (east + neighbour(1, 0, -1) + neighbour(1, 1, 0) + neighbour(1, 1, -1))
    res_east = (
        tendency(east, angular)
        + LINEAR_DRAG * east
        - rotation * north_mean
        + GRAVITY * (neighbour(0, 0, 1) - height)
    )
    res_north = (
        tendency(north, angular)
        + LINEAR_DRAG * north
        + rotation * east_mean
        + GRAVITY * (neighbour(0, 1, 0) - height)
    )
    return jnp.stack([res_height, res_east, res_north])


def friction_row(row_block, drag_row, table):
    highest = lax.Precision.HIGHEST
    series = jnp.einsum("tc,fcn->ftn", table, row_block, precision=highest)
    base_east, base_north, step_east, step_north = (series[0], series[1], series[2], series[3])
    magnitude = jnp.sqrt(base_east * base_east + base_north * base_north + SPEED_SOFT)
    projected = (base_east * step_east + base_north * step_north) / magnitude
    force_east = drag_row * (magnitude * step_east + base_east * projected)
    force_north = drag_row * (magnitude * step_north + base_north * projected)
    forces = jnp.stack([force_east, force_north])
    analysed = jnp.einsum("tc,ftn->fcn", table, forces, precision=highest) * (2.0 / table.shape[0])
    drag_rate = drag_row * jnp.mean(magnitude, axis=0)
    return (analysed, drag_rate)


def precondition(residual, angular, rotation, drag_rate):
    shaped = residual.reshape((3, residual.shape[1] // 2, 2) + residual.shape[2:])
    cos_part = shaped[:, :, 0]
    sin_part = shaped[:, :, 1]
    height_cos = -sin_part[0] / angular
    height_sin = cos_part[0] / angular
    real_rate = drag_rate + LINEAR_DRAG
    det_real = real_rate * real_rate - angular * angular + rotation * rotation
    det_imag = 2.0 * real_rate * angular
    det_norm = det_real * det_real + det_imag * det_imag
    inv_real = det_real / det_norm
    inv_imag = -det_imag / det_norm
    east_re = cos_part[1]
    east_im = -sin_part[1]
    north_re = cos_part[2]
    north_im = -sin_part[2]
    num_east_re = real_rate * east_re - angular * east_im + rotation * north_re
    num_east_im = real_rate * east_im + angular * east_re + rotation * north_im
    num_north_re = -rotation * east_re + real_rate * north_re - angular * north_im
    num_north_im = -rotation * east_im + real_rate * north_im + angular * north_re
    east_out_re = num_east_re * inv_real - num_east_im * inv_imag
    east_out_im = num_east_re * inv_imag + num_east_im * inv_real
    north_out_re = num_north_re * inv_real - num_north_im * inv_imag
    north_out_im = num_north_re * inv_imag + num_north_im * inv_real
    cosines = jnp.stack([height_cos, east_out_re, north_out_re])
    sines = jnp.stack([height_sin, -east_out_im, -north_out_im])
    return jnp.stack([cosines, sines], axis=2).reshape(residual.shape)


def local(direction, base_flow, water_depth, drag_factor, wet_mask):
    local_coefs = direction.shape[1]
    tile_rows = direction.shape[2]
    tile_cols = direction.shape[3]
    groups = lax.axis_size("freq")
    member = lax.axis_index("freq")
    band_rows = tile_rows // groups
    lat_place = lax.axis_index("lat")
    lat_count = lax.axis_size("lat")
    total_rows = tile_rows * lat_count
    wet_cells = wet_mask.astype(jnp.float32)
    height = direction[0] * wet_cells
    east = direction[1] * wet_cells
    north = direction[2] * wet_cells
    planes = jnp.stack([height, east, north, water_depth * east, water_depth * north])
    extended = extended_2(planes, (("lat", 2), ("lon", 3)), 1)
    rim_keep = jnp.ones((tile_rows + 2,), jnp.float32)
    rim_keep = rim_keep.at[0].set(jnp.where(lat_place == 0, 0.0, 1.0))
    rim_keep = rim_keep.at[tile_rows + 1].set(jnp.where(lat_place == lat_count - 1, 0.0, 1.0))
    extended = extended * rim_keep[:, None]
    local_count = local_coefs // 2
    first_con = member * local_count
    angular_local = OMEGA_STEP * (first_con + jnp.arange(local_count, dtype=jnp.int32) + 1).astype(
        jnp.float32
    )
    row_global = lat_place * tile_rows + jnp.arange(tile_rows, dtype=jnp.int32)
    rotation = rotation_of(row_global, total_rows)
    linear_part = linear_residual(
        extended, tile_rows, tile_cols, angular_local[:, None, None], rotation[:, None]
    )
    table = samples_table(NTIME, NCON)
    flows = jnp.concatenate([base_flow, jnp.stack([east, north])], axis=0)
    band_start = member * band_rows
    drag_band = lax.dynamic_slice_in_dim(drag_factor, band_start, band_rows, 0)
    flows_band, linear_band = (
        lax.all_to_all(flows, "freq", split_axis=2, concat_axis=1, tiled=True),
        lax.all_to_all(linear_part, "freq", split_axis=2, concat_axis=1, tiled=True),
    )
    mask_band = lax.dynamic_slice_in_dim(wet_cells, band_start, band_rows, 0)
    rotation_band = rotation_of(
        lat_place * tile_rows + band_start + jnp.arange(band_rows, dtype=jnp.int32), total_rows
    )
    angular_all = OMEGA_STEP * jnp.arange(1, NCON + 1, dtype=jnp.float32)

    def finish_row(items):
        row_block, linear_row, drag_row, mask_row, rotation_row = items
        friction, drag_rate = friction_row(row_block, drag_row, table)
        residual = (
            linear_row + jnp.concatenate([jnp.zeros_like(friction[:1]), friction], axis=0)
        ) * mask_row
        return precondition(residual, angular_all[:, None], rotation_row, drag_rate)

    band_result = lax.map(
        finish_row,
        (
            jnp.moveaxis(flows_band, 2, 0),
            jnp.moveaxis(linear_band, 2, 0),
            drag_band,
            mask_band,
            rotation_band,
        ),
    )
    band_result = jnp.moveaxis(band_result, 0, 2)
    return lax.all_to_all(band_result, "freq", split_axis=1, concat_axis=2, tiled=True)


def solution(mesh):
    placed = (
        P(None, "freq", "lat", "lon"),
        P(None, "freq", "lat", "lon"),
        P("lat", "lon"),
        P("lat", "lon"),
        P("lat", "lon"),
    )
    return jax.shard_map(
        local, mesh=mesh, in_specs=placed, out_specs=P(None, "freq", "lat", "lon"), check_vma=False
    )
```

profile of v0, /device:TPU:2, one launch (start us, length us, event | category | flops | bytes accessed | tf_op | source)
XLA Modules:
  0.0 540.5 jit_solution(4843827294149295579)
XLA Ops:
  8.5 3.3 collective-permute-start
  26.5 5.9 %maximum_multiply_fusion = f32[5,4,130,514]{3,2,1,0:T(8,128)S(1)} fusion(f32[5,4,130,1]{3,2,1,0:T(8,128)S(1)} %copy.113, f32[5,4,1,512]{3,2,1,0:T(1,128)S(1)} %copy.109, f32[5,4,128,512]{3,2,1,0:T(8,128)} %copy-done, f32[5,4,1,512]{3,2,1,0:T(1,128)S(1)} %copy.108, f32[5,4,130,1]{3,2,1,0:T(8,128)S(1)} %copy.112, f32[130]{0:T(256)S(1)} %constant_dynamic-update-slice_fusion.2), kind=kLoop, calls=%fused_computation.57 | loop fusion | flops 6682000 | bytes 10691720 | tf_op jit(solution)/shard_map/mul | solution.py:147
  38.4 3.7 copy.114
  42.1 8.5 %all-to-all-start = ((f32[3,4,128,512]{3,1,0,2:T(4,128)}), f32[3,4,128,512]{3,1,0,2:T(4,128)S(1)}, u32[]{:S(2)}, u32[]{:S(2)}) async-start(f32[3,4,128,512]{3,1,0,2:T(4,128)} %copy.114), calls=%async_computation | async-start | bytes 6291456 | tf_op jit(solution)/shard_map/all_to_all | solution.py:164
  58.5 66.9 %all-to-all-done = f32[3,4,128,512]{3,1,0,2:T(4,128)S(1)} async-done(((f32[3,4,128,512]{3,1,0,2:T(4,128)}), f32[3,4,128,512]{3,1,0,2:T(4,128)S(1)}, u32[]{:S(2)}, u32[]{:S(2)}) %all-to-all-start) | async-done | bytes 3145760 | tf_op jit(solution)/shard_map/all_to_all | solution.py:164
  125.5 4.6 all-to-all-start.1
  133.8 4.9 all_to_all.42
  138.7 88.1 %all-to-all-done.1 = f32[4,4,128,512]{3,1,0,2:T(4,128)} async-done(((f32[4,4,128,512]{3,1,0,2:T(4,128)}), f32[4,4,128,512]{3,1,0,2:T(4,128)}, u32[]{:S(2)}, u32[]{:S(2)}) %all-to-all-start.1) | async-done | bytes 4194336 | tf_op jit(solution)/shard_map/all_to_all | solution.py:163
  226.8 5.4 %copy.119 = f32[4,8,4,16,512]{4,2,1,0,3:T(4,128)} copy(f32[4,8,4,16,512]{4,2,0,3,1:T(4,128)} %bitcast.12) | data formatting | bytes 8388608 | tf_op jit(solution)/shard_map/all_to_all | solution.py:163
  232.2 5.3 all_to_all.46
  237.5 225.6 %while.15 = (s32[]{:T(128)}, f32[16,3,32,512]{3,0,1,2:T(8,128)}, f32[16,3,32,512]{3,2,1,0:T(8,128)}, f32[16,512]{1,0:T(8,128)S(1)}, f32[16,4,32,512]{3,2,1,0:T(8...) while((s32[]{:T(128)}, f32[16,3,32,512]{3,0,1,2:T(8,128)}, ...), condition=%wide.region_2.3_spmd.clone.clone, body=%wide.region_0.0_spmd.clone.clone.sunk | while | flops 305752128 | bytes 11770913 | solution.py:180
  237.5 2.9 convolution_bitcast_fusion.2
  246.6 5.0 dynamic_update_slice.8
  251.6 2.9 convolution_bitcast_fusion.2
  260.7 5.0 dynamic_update_slice.8
  265.7 2.9 convolution_bitcast_fusion.2
  274.8 5.0 dynamic_update_slice.8
  279.8 2.9 convolution_bitcast_fusion.2
  288.9 5.0 dynamic_update_slice.8
  303.0 5.0 dynamic_update_slice.8
  317.1 5.0 dynamic_update_slice.8
  331.2 5.0 dynamic_update_slice.8
  345.3 5.0 dynamic_update_slice.8
  359.4 5.0 dynamic_update_slice.8
  373.5 5.0 dynamic_update_slice.8
  387.5 5.0 dynamic_update_slice.8
  401.6 5.0 dynamic_update_slice.8
  415.7 5.0 dynamic_update_slice.8
  429.8 5.0 dynamic_update_slice.8
  443.9 5.0 dynamic_update_slice.8
  458.0 5.0 dynamic_update_slice.8
  463.0 75.5 %all_to_all.54 = f32[3,32,16,512]{3,2,0,1:T(8,128)S(1)} all-to-all(f32[3,32,16,512]{3,2,0,1:T(8,128)} %bitcast.160), channel_id=1, replica_groups=mesh['freq'=8,'lat'=8,'lon'=4] {'freq'}, dimensions={1} | all-to-all | bytes 6291456 | tf_op jit(solution)/shard_map/all_to_all | solution.py:191
  (376 shorter events, 147.9 us)
Async XLA Ops:
  2.3 3.4 copy-start.4
  3.9 2.2 copy-start.1
  5.7 2.7 copy-start.2
  6.0 2.4 copy-start
  8.5 6.7 %collective-permute-start = (f32[5,4,1,512]{3,0,2,1:T(8,128)S(1)}, f32[5,4,1,512]{3,0,2,1:T(8,128)S(1)}, u32[]{:S(2)}, u32[]{:S(2)}) collective-permute-start(f32[5,4,1,512]{3,0,2,1:T(8,128)S(1)} %copy.106), channel_id=1, source_target_pairs={{0,4},{4,8},{8,12},{12,16},{16,20},{20,24},{24,28},{28,0},{1,5},{5... | collective-permute-start | bytes 122888 | tf_op jit(solution)/shard_map/ppermute | solution.py:21
  11.8 5.8 %collective-permute-start.1 = (f32[5,4,1,512]{3,0,2,1:T(8,128)S(1)}, f32[5,4,1,512]{3,0,2,1:T(8,128)S(1)}, u32[]{:S(2)}, u32[]{:S(2)}) collective-permute-start(f32[5,4,1,512]{3,0,2,1:T(8,128)S(1)} %copy.107), channel_id=1, source_target_pairs={{4,0},{8,4},{12,8},{16,12},{20,16},{24,20},{28,24},{0,28},{5,1},{9... | collective-permute-start | bytes 122888 | tf_op jit(solution)/shard_map/ppermute | solution.py:24
  21.2 3.4 collective-permute-start.2
  22.4 3.6 collective-permute-start.3
  42.1 83.4 %all-to-all-start = ((f32[3,4,128,512]{3,1,0,2:T(4,128)}), f32[3,4,128,512]{3,1,0,2:T(4,128)S(1)}, u32[]{:S(2)}, u32[]{:S(2)}) async-start(f32[3,4,128,512]{3,1,0,2:T(4,128)} %copy.114), calls=%async_computation | async-start | bytes 6291456 | tf_op jit(solution)/shard_map/all_to_all | solution.py:164
  50.6 4.0 copy-start.3
  125.5 101.3 %all-to-all-start.1 = ((f32[4,4,128,512]{3,1,0,2:T(4,128)}), f32[4,4,128,512]{3,1,0,2:T(4,128)}, u32[]{:S(2)}, u32[]{:S(2)}) async-start(f32[4,4,128,512]{3,1,0,2:T(4,128)} %pad_maximum_fusion.1), calls=%async_computation.1 | async-start | bytes 8388608 | tf_op jit(solution)/shard_map/all_to_all | solution.py:163
where the time goes:
time: 544 us; the launch traced here: 541 us
  waiting for transfers between devices  161 us (30%)
  local copies, waits for them, and re-layouts  136 us (25%)
  blocking collectives  75.5 us (14%)
  other arithmetic  61.9 us (11%)
  matrix products  57.8 us (11%)
  loops' own time  29.1 us (5%)
  starting transfers between devices  19.6 us (4%)
    all_to_all x1, waiting for transfers between devices, local(): lax.all_to_all(flows, 'freq', split_axis=2, concat_axis=1, tiled=True)  88.1 us
    dynamic_update_slice x48, local copies, waits for them, and re-layouts, local(): lax.map(finish_row, (jnp.moveaxis(flows_band, 2, 0), jnp.moveaxis(linear_...  86.2 us
    all_to_all x1, blocking collectives, local(): lax.all_to_all(band_result, 'freq', split_axis=1, concat_axis=2, tiled=True)  75.5 us
    all_to_all x1, waiting for transfers between devices, local(): lax.all_to_all(linear_part, 'freq', split_axis=2, concat_axis=1, tiled=True)  66.9 us
    dot_general x16, matrix products, friction_row(): series = jnp.einsum('tc,fcn->ftn', table, row_block, precision=highest)  46.2 us
    another operation x1, loops' own time, local(): lax.map(finish_row, (jnp.moveaxis(flows_band, 2, 0), jnp.moveaxis(linear_...  29.1 us
    mul x16, other arithmetic, finish_row(): (linear_row + jnp.concatenate([jnp.zeros_like(friction[:1]), friction], a...  15.4 us
    dot_general x16, matrix products, friction_row(): jnp.einsum('tc,ftn->fcn', table, forces, precision=highest)  11.7 us
  transfers between devices with their start and end apart: 6, of which 6 were waited for; matrix products, arithmetic and copies ran while one was open for 2% of the time, Pallas kernels for 0%

commit v1 on v0

--- a/solution.py
+++ b/solution.py
@@ -10,6 +10,14 @@
 GRAVITY = 1.0
 OMEGA_STEP = 0.25
 SPEED_SOFT = 0.01
+
+
+def press_bars(xs, on_dim, row_dim):
+    prior = lax.axis_size("freq")
+    d_next = jnp.split(xs, prior, axis=on_dim)
+    reply = jnp.stack(d_next, axis=0)
+    view_out = lax.all_to_all(reply, axis_name="freq", split_axis=0, concat_axis=0)
+    return jnp.concatenate(view_out, axis=row_dim)
 
 
 def extended_2(block, sides, width):
@@ -188,7 +196,7 @@
         ),
     )
     band_result = jnp.moveaxis(band_result, 0, 2)
-    return lax.all_to_all(band_result, "freq", split_axis=1, concat_axis=2, tiled=True)
+    return press_bars(band_result, 1, 2)
 
 
 def solution(mesh):

time: 544 us -> 494 us (0.908)
  local copies, waits for them, and re-layouts: 136 us -> 71.6 us
  matrix products: 57.8 us -> 70 us
    dynamic_update_slice x48 -> x16, local copies, waits for them, and re-layouts: 86.2 us -> 11.1 us  [local(): lax.map(finish_row, (jnp.moveaxis(flows_band, 2, 0), jnp.moveaxis(linear_...]
    mul x16, other arithmetic: 15.4 us -> 0.49 us  [finish_row(): (linear_row + jnp.concatenate([jnp.zeros_like(friction[:1]), friction], a...]
    dot_general x16, matrix products: 11.7 us -> 23.8 us  [friction_row(): jnp.einsum('tc,ftn->fcn', table, forces, precision=highest)]
    mul x16, other arithmetic: 0.29 us -> 12 us  [precondition(): det_real = real_rate * real_rate - angular * angular + rotation * rotation]
  transfers between devices with their start and end apart: 6 -> 6, of which waited for: 6 -> 6; matrix products, arithmetic and copies ran while one was open for 2% -> 3% of each run, Pallas kernels for 0% -> 0%
where the time goes in v1:
time: 494 us; the launch traced here: 490 us
  waiting for transfers between devices  161 us (33%)
  blocking collectives  75.3 us (15%)
  local copies, waits for them, and re-layouts  71.6 us (14%)
  matrix products  70 us (14%)
  other arithmetic  59.8 us (12%)
  loops' own time  32.2 us (7%)
  starting transfers between devices  19.6 us (4%)
    all_to_all x1, waiting for transfers between devices, local(): lax.all_to_all(flows, 'freq', split_axis=2, concat_axis=1, tiled=True)  88.6 us
    all_to_all x1, blocking collectives, press_bars(): lax.all_to_all(reply, axis_name='freq', split_axis=0, concat_axis=0)  75.3 us
    all_to_all x1, waiting for transfers between devices, local(): lax.all_to_all(linear_part, 'freq', split_axis=2, concat_axis=1, tiled=True)  66.9 us
    dot_general x16, matrix products, friction_row(): series = jnp.einsum('tc,fcn->ftn', table, row_block, precision=highest)  46.2 us
    another operation x1, loops' own time, local(): lax.map(finish_row, (jnp.moveaxis(flows_band, 2, 0), jnp.moveaxis(linear_...  32.2 us
    dot_general x16, matrix products, friction_row(): jnp.einsum('tc,ftn->fcn', table, forces, precision=highest)  23.8 us
    mul x16, other arithmetic, precondition(): det_real = real_rate * real_rate - angular * angular + rotation * rotation  12 us
    sub x16, other arithmetic, precondition(): east_out_re = num_east_re * inv_real - num_east_im * inv_imag  11.7 us
  transfers between devices with their start and end apart: 6, of which 6 were waited for; matrix products, arithmetic and copies ran while one was open for 3% of the time, Pallas kernels for 0%

profile of v1, /device:TPU:2, one launch (start us, length us, event | category | flops | bytes accessed | tf_op | source)
XLA Modules:
  0.0 489.9 jit_solution(18152999448794091365)
XLA Ops:
  8.5 3.3 collective-permute-start
  26.5 5.9 %maximum_multiply_fusion = f32[5,4,130,514]{3,2,1,0:T(8,128)S(1)} fusion(f32[5,4,130,1]{3,2,1,0:T(8,128)S(1)} %copy.109, f32[5,4,1,512]{3,2,1,0:T(1,128)S(1)} %copy.105, f32[5,4,128,512]{3,2,1,0:T(8,128)} %copy-done, f32[5,4,1,512]{3,2,1,0:T(1,128)S(1)} %copy.104, f32[5,4,130,1]{3,2,1,0:T(8,128)S(1)} %copy.108, f32[130]{0:T(256)S(1)} %constant_dynamic-update-slice_fusion.3), kind=kLoop, calls=%fused_computation.58 | loop fusion | flops 6682000 | bytes 10691720 | tf_op jit(solution)/shard_map/mul | solution.py:155
  35.4 2.7 fusion.27
  38.4 3.7 copy.110
  42.1 8.5 %all-to-all-start = ((f32[3,4,128,512]{3,1,0,2:T(4,128)}), f32[3,4,128,512]{3,1,0,2:T(4,128)S(1)}, u32[]{:S(2)}, u32[]{:S(2)}) async-start(f32[3,4,128,512]{3,1,0,2:T(4,128)} %copy.110), calls=%async_computation | async-start | bytes 6291456 | tf_op jit(solution)/shard_map/all_to_all | solution.py:172
  55.9 2.7 pad_maximum_fusion.1
  58.6 66.9 %all-to-all-done = f32[3,4,128,512]{3,1,0,2:T(4,128)S(1)} async-done(((f32[3,4,128,512]{3,1,0,2:T(4,128)}), f32[3,4,128,512]{3,1,0,2:T(4,128)S(1)}, u32[]{:S(2)}, u32[]{:S(2)}) %all-to-all-start) | async-done | bytes 3145760 | tf_op jit(solution)/shard_map/all_to_all | solution.py:172
  125.5 4.6 all-to-all-start.1
  132.3 2.7 copy.111
  134.9 3.2 all_to_all.32
  138.1 88.6 %all-to-all-done.1 = f32[4,4,128,512]{3,1,0,2:T(4,128)} async-done(((f32[4,4,128,512]{3,1,0,2:T(4,128)}), f32[4,4,128,512]{3,1,0,2:T(4,128)}, u32[]{:S(2)}, u32[]{:S(2)}) %all-to-all-start.1) | async-done | bytes 4194336 | tf_op jit(solution)/shard_map/all_to_all | solution.py:171
  226.8 5.4 %copy.115 = f32[4,8,4,16,512]{4,2,1,0,3:T(4,128)} copy(f32[4,8,4,16,512]{4,2,0,3,1:T(4,128)} %bitcast.12) | data formatting | bytes 8388608 | tf_op jit(solution)/shard_map/all_to_all | solution.py:171
  232.2 5.3 %all_to_all.36 = f32[4,32,16,512]{3,1,0,2:T(8,128)} reshape(f32[4,8,4,16,512]{4,2,1,0,3:T(4,128)} %copy.115) | data formatting | bytes 8388608 | tf_op jit(solution)/shard_map/all_to_all | solution.py:171
  237.5 169.0 %while.15 = (s32[]{:T(128)}, f32[16,3,32,512]{3,2,1,0:T(8,128)}, f32[16,3,32,512]{3,2,1,0:T(8,128)S(1)}, f32[16,512]{1,0:T(8,128)}, f32[16,4,32,512]{3,2,1,0:T(8...) while((s32[]{:T(128)}, f32[16,3,32,512]{3,2,1,0:T(8,128)}, ...), condition=%wide.region_2.3_spmd.clone.clone, body=%wide.region_0.0_spmd.clone.clone.sunk | while | flops 305752128 | bytes 11771413 | solution.py:188
  237.5 2.9 convolution_bitcast_fusion.2
  248.0 2.9 convolution_bitcast_fusion.2
  258.6 2.9 convolution_bitcast_fusion.2
  269.1 2.9 convolution_bitcast_fusion.2
  279.7 2.9 convolution_bitcast_fusion.2
  290.3 2.9 convolution_bitcast_fusion.2
  300.8 2.9 convolution_bitcast_fusion.2
  311.4 2.9 convolution_bitcast_fusion.2
  321.9 2.9 convolution_bitcast_fusion.2
  332.5 2.9 convolution_bitcast_fusion.2
  343.1 2.9 convolution_bitcast_fusion.2
  353.6 2.9 convolution_bitcast_fusion.2
  364.2 2.9 convolution_bitcast_fusion.2
  374.7 2.9 convolution_bitcast_fusion.2
  385.3 2.9 convolution_bitcast_fusion.2
  395.9 2.9 convolution_bitcast_fusion.2
  411.9 75.3 %all_to_all.41 = f32[8,3,4,16,512]{4,2,1,3,0:T(4,128)S(1)} all-to-all(f32[8,3,4,16,512]{4,2,1,3,0:T(4,128)S(1)} %fusion.30), channel_id=1, replica_groups=mesh['freq'=8,'lat'=8,'lon'=4] {'freq'}, dimensions={0} | all-to-all | bytes 6291456 | tf_op jit(solution)/shard_map/all_to_all | solution.py:19
  487.3 2.6 copy.117
  (386 shorter events, 129.9 us)
Async XLA Ops:
  2.3 3.4 copy-start.5
  3.9 2.2 copy-start.1
  5.7 2.7 copy-start.2
  6.0 2.4 copy-start
  8.5 6.7 %collective-permute-start = (f32[5,4,1,512]{3,0,2,1:T(8,128)S(1)}, f32[5,4,1,512]{3,0,2,1:T(8,128)S(1)}, u32[]{:S(2)}, u32[]{:S(2)}) collective-permute-start(f32[5,4,1,512]{3,0,2,1:T(8,128)S(1)} %copy.102), channel_id=1, source_target_pairs={{0,4},{4,8},{8,12},{12,16},{16,20},{20,24},{24,28},{28,0},{1,5},{5... | collective-permute-start | bytes 122888 | tf_op jit(solution)/shard_map/ppermute | solution.py:29
  11.8 5.8 %collective-permute-start.1 = (f32[5,4,1,512]{3,0,2,1:T(8,128)S(1)}, f32[5,4,1,512]{3,0,2,1:T(8,128)S(1)}, u32[]{:S(2)}, u32[]{:S(2)}) collective-permute-start(f32[5,4,1,512]{3,0,2,1:T(8,128)S(1)} %copy.103), channel_id=1, source_target_pairs={{4,0},{8,4},{12,8},{16,12},{20,16},{24,20},{28,24},{0,28},{5,1},{9... | collective-permute-start | bytes 122888 | tf_op jit(solution)/shard_map/ppermute | solution.py:32
  21.2 3.4 collective-permute-start.2
  22.4 3.6 collective-permute-start.3
  42.1 83.4 %all-to-all-start = ((f32[3,4,128,512]{3,1,0,2:T(4,128)}), f32[3,4,128,512]{3,1,0,2:T(4,128)S(1)}, u32[]{:S(2)}, u32[]{:S(2)}) async-start(f32[3,4,128,512]{3,1,0,2:T(4,128)} %copy.110), calls=%async_computation | async-start | bytes 6291456 | tf_op jit(solution)/shard_map/all_to_all | solution.py:172
  50.6 4.0 copy-start.4
  125.5 101.3 %all-to-all-start.1 = ((f32[4,4,128,512]{3,1,0,2:T(4,128)}), f32[4,4,128,512]{3,1,0,2:T(4,128)}, u32[]{:S(2)}, u32[]{:S(2)}) async-start(f32[4,4,128,512]{3,1,0,2:T(4,128)} %pad_maximum_fusion.1), calls=%async_computation.1 | async-start | bytes 8388608 | tf_op jit(solution)/shard_map/all_to_all | solution.py:171
  406.4 5.1 %copy-start.3 = (f32[16,3,32,512]{3,2,1,0:T(8,128)S(1)}, f32[16,3,32,512]{3,2,1,0:T(8,128)}, u32[]{:S(2)}) copy-start(f32[16,3,32,512]{3,2,1,0:T(8,128)} %get-tuple-element.135) | copy-start | bytes 9437188
